TPU v7x, 32 devices: a whole 2x2x4 slice. The times are simulated.
32 devices in a mesh: tgt: 8 (over z, core), sup: 4 (over y, x).
Axes of the slice: x: 2, y: 2, z: 4, core: 2. Of those that a mesh axis runs over, the one named last changes fastest.
Arguments:
- target_pool: float32 [512, 3, 1024], P('tgt'), may hold values from -6 to 6
- target_index: int32 [64], P('tgt'), may hold values from 0 to 511, as said below
- target_labels: int32 [64], P('tgt'), may hold values from 0 to 99
- dual_weights: float32 [128, 100], P('sup'), may hold values from -0.5 to 0.5
- support_images: float32 [128, 3, 1024], P(('sup', 'tgt')), may hold values from -6 to 6
Outputs:
- residual: float32 [64, 100], P('tgt')
- support_grad: float32 [128, 3, 1024], P(('sup', 'tgt'))
Inputs may be any that keep to these rules, and one draw needn't show every extreme that they name: `target_index`: for each j, the targets 8 * j to 8 * (j + 1) - 1 name distinct candidates among 64 * j to 64 * (j + 1) - 1.
All inputs are finite; a program needn't handle non-finite values.
Results may differ from a plain program's by a relative error of at most 0.0003.
Values sent between devices are 32-bit elements; how exact they have to be, the bound alone decides.
A program may use at most 64 MiB of HBM per device.

v0:
```python
import math
import jax
import jax.numpy as jnp
from jax import lax
from jax.sharding import PartitionSpec as P

CHANNELS = 3
SIDE = 32
CLASSES = 100
LAYERS = 3
PIXELS = 1024
bias_variance = 0.01


def box_filter(pixel_map):
    column = jnp.arange(PIXELS) % SIDE
    zero_column = jnp.zeros(pixel_map.shape[:-1] + (1,), pixel_map.dtype)
    shifted_right = jnp.concatenate([zero_column, pixel_map[..., :-1]], axis=-1)
    shifted_left = jnp.concatenate([pixel_map[..., 1:], zero_column], axis=-1)
    across = (
        pixel_map
        + jnp.where(column > 0, shifted_right, 0.0)
        + jnp.where(column < SIDE - 1, shifted_left, 0.0)
    )
    zero_row = jnp.zeros(pixel_map.shape[:-1] + (SIDE,), pixel_map.dtype)
    shifted_down = jnp.concatenate([zero_row, across[..., :-SIDE]], axis=-1)
    shifted_up = jnp.concatenate([across[..., SIDE:], zero_row], axis=-1)
    return (across + shifted_down + shifted_up) / 9.0


def self_maps(images):
    energy = images[:, 0] * images[:, 0]
    for channel in range(1, CHANNELS):
        energy = energy + images[:, channel] * images[:, channel]
    current = box_filter(energy / CHANNELS) + bias_variance
    levels = [current]
    for layer_index in range(1, LAYERS):
        current = box_filter(current) + bias_variance
        levels.append(current)
    return levels


def rectified(cross, target_level, support_level):
    spread = jnp.sqrt(target_level * support_level - cross * cross)
    polar_angle = jnp.arctan2(spread, cross)
    return ((spread + (math.pi - polar_angle) * cross) / math.pi, spread, polar_angle)


def cross_forward(targets, support, target_levels, support_levels):
    inner_sum = targets[:, None, 0] * support[None, :, 0]
    for channel in range(1, CHANNELS):
        inner_sum = inner_sum + targets[:, None, channel] * support[None, :, channel]
    cross = box_filter(inner_sum / CHANNELS) + bias_variance
    saved_maps = []
    output_map = cross
    for layer_index in range(LAYERS):
        output_map, spread, polar_angle = rectified(
            cross, target_levels[layer_index][:, None], support_levels[layer_index][None]
        )
        saved_maps.append((spread, polar_angle))
        if layer_index + 1 < LAYERS:
            cross = box_filter(output_map) + bias_variance
    return (jnp.mean(output_map, axis=-1), saved_maps)


def cross_backward(weight, saved_maps, targets, support, support_levels):
    upstream = weight[:, :, None]
    level_grad = None
    for layer_index in range(LAYERS - 1, -1, -1):
        spread, polar_angle = saved_maps[layer_index]
        level_term = jnp.sum(upstream * spread, axis=0) / (
            2.0 * math.pi * support_levels[layer_index]
        )
        level_grad = level_term if level_grad is None else level_term + box_filter(level_grad)
        upstream = box_filter(upstream * (math.pi - polar_angle) / math.pi)
    energy_grad = box_filter(level_grad) / CHANNELS
    channel_grads = []
    for channel in range(CHANNELS):
        carried = jnp.sum(upstream * targets[:, None, channel], axis=0) / CHANNELS
        channel_grads.append(carried + 2.0 * support[:, channel] * energy_grad)
    return jnp.stack(channel_grads, axis=1)


def shards(target_pool, target_index, target_labels, dual_weights, support_images):
    local_rows = target_index - lax.axis_index("tgt") * target_pool.shape[0]
    targets = jnp.take(target_pool, local_rows, axis=0)
    onehot = (target_labels[:, None] == jnp.arange(CLASSES)[None, :]).astype(jnp.float32)
    own_count = support_images.shape[0]
    all_targets, all_onehot = (
        lax.all_gather(targets, "tgt", axis=0, tiled=True),
        lax.all_gather(onehot, "tgt", axis=0, tiled=True),
    )
    own_duals = lax.dynamic_slice_in_dim(
        dual_weights, lax.axis_index("tgt") * own_count, own_count, 0
    )
    support_levels = self_maps(support_images)
    kernel, saved_maps = cross_forward(
        all_targets, support_images, self_maps(all_targets), support_levels
    )
    partial_value = jnp.dot(
        kernel, own_duals, precision=lax.Precision.HIGHEST, preferred_element_type=jnp.float32
    )
    predicted = lax.psum(partial_value, ("tgt", "sup"))
    residual_all = predicted - all_onehot
    weight = jnp.dot(
        residual_all,
        own_duals.T,
        precision=lax.Precision.HIGHEST,
        preferred_element_type=jnp.float32,
    )
    support_grad = cross_backward(weight, saved_maps, all_targets, support_images, support_levels)
    residual = lax.dynamic_slice_in_dim(
        residual_all, lax.axis_index("tgt") * targets.shape[0], targets.shape[0], 0
    )
    return (residual, support_grad)


def solution(mesh):
    in_specs = (
        P("tgt", None, None),
        P("tgt"),
        P("tgt"),
        P("sup", None),
        P(("sup", "tgt"), None, None),
    )
    out_specs = (P("tgt", None), P(("sup", "tgt"), None, None))
    return jax.shard_map(shards, mesh=mesh, in_specs=in_specs, out_specs=out_specs, check_vma=False)
```

profile of v0, /device:TPU:0, one launch (start us, length us, event | category | flops | bytes accessed | tf_op | source)
XLA Modules:
  0.0 109.1 jit_solution(5623943175997622236)
XLA Ops:
  0.7 0.7 copy-done.9
  1.4 0.4 copy-done
  1.8 0.7 gather_fusion
  2.6 17.2 %all_gather.6 = f32[64,3,1024]{2,0,1:T(8,128)S(1)} all-gather(f32[8,3,1024]{2,0,1:T(8,128)S(1)} %broadcast_select_fusion), channel_id=1, replica_groups=mesh['tgt'=8,'sup'=4] {'tgt'}, dimensions={0}, use_global_device_ids=true | all-gather | bytes 884736 | tf_op jit(solution)/shard_map/all_gather | solution.py:90
  19.8 0.9 broadcast_multiply_fusion.1
  20.8 0.1 select_add_fusion.8
  21.1 0.1 multiply_add_fusion.5
  21.3 0.7 copy-done.6
  22.1 0.2 add_multiply_fusion.4
  22.3 0.4 fusion.26
  22.7 0.5 select_add_fusion.5
  23.2 0.4 fusion.25
  23.9 2.3 %add_multiply_fusion.3 = (f32[64,4,1024]{2,0,1:T(8,128)S(1)}, f32[64,4,1024]{2,0,1:T(8,128)S(1)}) fusion(f32[4,1024]{1,0:T(4,128)S(1)} %multiply_add_fusion.10, f32[64,1024]{1,0:T(8,128)S(1)} %multiply_add_fusion.5, f32[64,4,992]{2,0,1:T(8,128)S(1)} %get-tuple-element.42, f32[64,4,1024]{2,0,1:T(8,128)S(1)} %select_add_fusion.5, ...), kind=kLoop, calls=%fused_computation.26 | loop fusion | flops 2883584 | bytes 5455872 | tf_op jit(solution)/shard_map/div | solution.py:46
  26.2 0.4 fusion.24
  26.6 0.5 select_add_fusion.4
  27.1 0.4 fusion.23
  27.6 0.1 select_add_fusion.7
  27.7 0.1 fusion.29
  27.9 0.1 multiply_add_fusion.4
  28.3 3.2 %add_multiply_fusion.2 = (f32[64,4,1024]{2,0,1:T(8,128)S(1)}, f32[64,4,1024]{2,0,1:T(8,128)}) fusion(f32[4,1024]{1,0:T(4,128)S(1)} %multiply_add_fusion.9, f32[64,1024]{1,0:T(8,128)S(1)} %multiply_add_fusion.4, f32[64,4,992]{2,0,1:T(8,128)S(1)} %get-tuple-element.38, f32[64,4,1024]{2,0,1:T(8,128)S(1)} %select_add_fusion.4, ...), kind=kLoop, calls=%fused_computation.21 | loop fusion | flops 2883584 | bytes 5455872 | tf_op jit(solution)/shard_map/div | solution.py:46
  31.5 0.4 fusion.22
  31.9 0.4 select_add_fusion.3
  32.4 0.4 fusion.21
  32.9 0.1 select_add_fusion.6
  33.1 0.1 fusion.27
  33.2 0.1 multiply_add_fusion.3
  33.7 2.7 %multiply_reduce_fusion.6 = (f32[64,4]{0,1:T(4,128)S(1)}, f32[64,4,1024]{2,0,1:T(8,128)S(1)}) fusion(f32[4,1024]{1,0:T(4,128)S(1)} %multiply_add_fusion.8, f32[64,1024]{1,0:T(8,128)S(1)} %multiply_add_fusion.3, f32[64,4,992]{2,0,1:T(8,128)S(1)} %get-tuple-element.34, f32[64,4,1024]{2,0,1:T(8,128)S(1)} %select_add_fusion.3, ...), kind=kLoop, calls=%fused_computation.16 | loop fusion | flops 3145472 | bytes 4408320 | tf_op jit(solution)/shard_map/reduce_sum | solution.py:63
  36.4 0.9 fusion.6
  37.3 40.9 %psum.7 = f32[64,100]{1,0:T(8,128)} all-reduce(f32[64,100]{1,0:T(8,128)S(1)} %fusion.6), channel_id=1, replica_groups=mesh['tgt'=8,'sup'=4] {'tgt','sup'}, use_global_device_ids=true, to_apply=%region_1.2 | all-reduce | flops 6400 | bytes 51200 | tf_op jit(solution)/shard_map/psum | solution.py:103
  78.3 14.2 %all_gather.7 = f32[64,100]{1,0:T(8,128)S(1)} all-gather(f32[8,100]{1,0:T(8,128)S(1)} %fusion.5), channel_id=1, replica_groups=mesh['tgt'=8,'sup'=4] {'tgt'}, dimensions={0}, use_global_device_ids=true | all-gather | bytes 28800 | tf_op jit(solution)/shard_map/all_gather | solution.py:91
  92.5 0.8 fusion.8
  93.4 3.1 %multiply_reduce_fusion.2 = (f32[4,1024]{1,0:T(4,128)S(1)}, f32[64,4,1024]{2,0,1:T(8,128)S(1)}) fusion(f32[64,4,1024]{2,0,1:T(8,128)S(1)} %get-tuple-element.8, f32[64,4]{0,1:T(4,128)S(1)} %fusion.8, f32[4,1024]{1,0:T(4,128)S(1)} %multiply_add_fusion.8, f32[64,1024]{1,0:T(8,128)} %copy-done.2), kind=kLoop, calls=%fused_computation.3 | loop fusion | flops 2093056 | bytes 2393088 | tf_op jit(solution)/shard_map/reduce_sum | solution.py:71
  96.7 0.4 fusion.20
  97.1 0.4 select_add_fusion.2
  97.5 0.4 fusion.19
  97.9 0.8 copy-done.1
  98.7 2.3 %multiply_reduce_fusion.3 = (f32[4,1024]{1,0:T(4,128)S(1)}, f32[64,4,1024]{2,0,1:T(8,128)S(1)}) fusion(f32[64,4,1024]{2,0,1:T(8,128)S(1)} %copy-done.1, f32[4,1024]{1,0:T(4,128)S(1)} %multiply_add_fusion.9, f32[64,1024]{1,0:T(8,128)S(1)} %multiply_add_fusion.4, f32[64,4,992]{2,0,1:T(8,128)S(1)} %get-tuple-element.30, f32[64,4,1024]{2,0,1:T(8,128)S(1)} %select_add_fusion.2, ...), kind=kLoop, calls=%fused_computation.4 | loop fusion | flops 2879488 | bytes 5472256 | tf_op jit(solution)/shard_map/reduce_sum | solution.py:71
  101.4 0.4 fusion.18
  101.8 0.4 select_add_fusion.1
  102.2 0.4 fusion.17
  102.6 2.3 %multiply_reduce_fusion.4 = (f32[4,1024]{1,0:T(4,128)S(1)}, f32[64,4,1024]{2,0,1:T(8,128)S(1)}) fusion(f32[64,4,1024]{2,0,1:T(8,128)S(1)} %get-tuple-element.12, f32[4,1024]{1,0:T(4,128)S(1)} %multiply_add_fusion.10, f32[64,1024]{1,0:T(8,128)S(1)} %multiply_add_fusion.5, f32[64,4,992]{2,0,1:T(8,128)S(1)} %get-tuple-element.26, ...), kind=kLoop, calls=%fused_computation.5 | loop fusion | flops 2879488 | bytes 5472256 | tf_op jit(solution)/shard_map/reduce_sum | solution.py:71
  105.2 0.4 fusion.16
  105.6 0.4 select_add_fusion
  106.1 0.4 fusion.15
  106.5 0.5 copy-done.3
  107.2 0.5 multiply_reduce_fusion.5
  107.9 0.6 pad_maximum_fusion
  108.5 0.6 constant_dynamic-slice_fusion
  (54 shorter events, 2.9 us)
Async XLA Ops:
  0.6 1.2 %copy-start = (f32[64,3,1024]{2,0,1:T(8,128)S(1)}, f32[64,3,1024]{2,0,1:T(8,128)}, u32[]{:S(2)}) copy-start(f32[64,3,1024]{2,0,1:T(8,128)} %param.5) | copy-start | bytes 2359300
  0.7 0.7 copy-start.9
  21.3 0.8 copy-start.6
  33.4 3.0 %copy-start.2 = (f32[64,1024]{1,0:T(8,128)}, f32[64,1024]{1,0:T(8,128)S(1)}, u32[]{:S(2)}) copy-start(f32[64,1024]{1,0:T(8,128)S(1)} %multiply_add_fusion.3) | copy-start | bytes 786436
  37.3 40.9 %copy-start.8 = (s32[8]{0:T(128)S(1)}, s32[8]{0:T(128)}, u32[]{:S(2)}) copy-start(s32[8]{0:T(128)} %param.7) | copy-start | bytes 100
  78.2 14.3 %copy-start.7 = (f32[64,100]{1,0:T(8,128)S(1)}, f32[64,100]{1,0:T(8,128)}, u32[]{:S(2)}) copy-start(f32[64,100]{1,0:T(8,128)} %psum.7) | copy-start | bytes 76804
  97.5 1.2 %copy-start.1 = (f32[64,4,1024]{2,0,1:T(8,128)S(1)}, f32[64,4,1024]{2,0,1:T(8,128)}, u32[]{:S(2)}) copy-start(f32[64,4,1024]{2,0,1:T(8,128)} %get-tuple-element.10) | copy-start | bytes 3145732
  106.1 1.0 copy-start.3
  106.1 1.0 copy-start.4
  106.1 1.1 %copy-start.5 = (f32[64,1024]{1,0:T(8,128)S(1)}, f32[64,1024]{1,0:T(8,128)}, u32[]{:S(2)}) copy-start(f32[64,1024]{1,0:T(8,128)} %get-tuple-element.48) | copy-start | bytes 786436
where the time goes:
time: 110 us; the launch traced here: 109 us
  blocking collectives  72.3 us (66%)
  other arithmetic  22.9 us (21%)
  local copies, waits for them, and re-layouts  11.1 us (10%)
  matrix products  1.75 us (2%)
    psum x1, blocking collectives, shards(): predicted = lax.psum(partial_value, ('tgt', 'sup'))  40.9 us
    all_gather x1, blocking collectives, shards(): lax.all_gather(targets, 'tgt', axis=0, tiled=True)  17.2 us
    all_gather x1, blocking collectives, shards(): lax.all_gather(onehot, 'tgt', axis=0, tiled=True)  14.2 us
    reduce_sum x3, other arithmetic, cross_backward(): jnp.sum(upstream * spread, axis=0)  7.66 us
    div x2, other arithmetic, rectified(): (spread + (math.pi - polar_angle) * cross) / math.pi  5.48 us
    add x15, other arithmetic, box_filter(): pixel_map + jnp.where(column > 0, shifted_right, 0.0)  3.66 us
    unnamed x20, local copies, waits for them, and re-layouts  3.37 us
    slice x15, local copies, waits for them, and re-layouts, box_filter(): shifted_right = jnp.concatenate([zero_column, pixel_map[..., :-1]], axis=-1)  3.19 us

commit v1 on v0

--- a/solution.py
+++ b/solution.py
@@ -100,7 +100,7 @@
     partial_value = jnp.dot(
         kernel, own_duals, precision=lax.Precision.HIGHEST, preferred_element_type=jnp.float32
     )
-    predicted = lax.psum(partial_value, ("tgt", "sup"))
+    predicted = jnp.sum(lax.all_gather(partial_value, ("tgt", "sup")), axis=0)
     residual_all = predicted - all_onehot
     weight = jnp.dot(
         residual_all,

time: 110 us -> 145 us (1.32)
  blocking collectives: 72.3 us -> 106 us
    all_gather x0 -> x1, blocking collectives: none -> 74.4 us  [shards(): predicted = jnp.sum(lax.all_gather(partial_value, ('tgt', 'sup')), axis=0)]
    psum x1 -> x0, blocking collectives: 40.9 us -> none  [shards(): predicted = lax.psum(partial_value, ('tgt', 'sup'))]
where the time goes in v1:
time: 145 us
  blocking collectives  106 us (73%)
  other arithmetic  23.9 us (16%)
  local copies, waits for them, and re-layouts  12.4 us (9%)
  matrix products  1.75 us (1%)
    all_gather x1, blocking collectives, shards(): predicted = jnp.sum(lax.all_gather(partial_value, ('tgt', 'sup')), axis=0)  74.4 us
    all_gather x1, blocking collectives, shards(): lax.all_gather(targets, 'tgt', axis=0, tiled=True)  17.2 us
    all_gather x1, blocking collectives, shards(): lax.all_gather(onehot, 'tgt', axis=0, tiled=True)  14.1 us
    reduce_sum x3, other arithmetic, cross_backward(): jnp.sum(upstream * spread, axis=0)  7.66 us
    div x2, other arithmetic, rectified(): (spread + (math.pi - polar_angle) * cross) / math.pi  6.39 us
    unnamed x20, local copies, waits for them, and re-layouts  4.76 us
    add x15, other arithmetic, box_filter(): pixel_map + jnp.where(column > 0, shifted_right, 0.0)  3.65 us
    slice x15, local copies, waits for them, and re-layouts, box_filter(): shifted_right = jnp.concatenate([zero_column, pixel_map[..., :-1]], axis=-1)  3.19 us

profile of v1, /device:TPU:0, one launch (start us, length us, event | category | flops | bytes accessed | tf_op | source)
XLA Modules:
  0.0 144.8 jit_solution(15433403463688709808)
XLA Ops:
  0.7 0.7 copy-done.9
  1.4 0.4 copy-done
  1.8 0.7 gather_fusion
  2.6 17.2 %all_gather.12 = f32[64,3,1024]{2,0,1:T(8,128)S(1)} all-gather(f32[8,3,1024]{2,0,1:T(8,128)S(1)} %broadcast_select_fusion), channel_id=1, replica_groups=mesh['tgt'=8,'sup'=4] {'tgt'}, dimensions={0}, use_global_device_ids=true | all-gather | bytes 884736 | tf_op jit(solution)/shard_map/all_gather | solution.py:90
  19.8 0.9 broadcast_multiply_fusion.1
  20.8 0.1 select_add_fusion.8
  21.1 0.1 multiply_add_fusion.5
  21.3 0.7 copy-done.7
  22.1 0.2 add_multiply_fusion.4
  22.3 0.4 fusion.26
  22.7 0.5 select_add_fusion.5
  23.2 0.4 fusion.25
  23.9 3.2 %add_multiply_fusion.3 = (f32[64,4,1024]{2,0,1:T(8,128)S(1)}, f32[64,4,1024]{2,0,1:T(8,128)}) fusion(f32[4,1024]{1,0:T(4,128)S(1)} %multiply_add_fusion.10, f32[64,1024]{1,0:T(8,128)S(1)} %multiply_add_fusion.5, f32[64,4,992]{2,0,1:T(8,128)S(1)} %get-tuple-element.42, f32[64,4,1024]{2,0,1:T(8,128)S(1)} %select_add_fusion.5, ...), kind=kLoop, calls=%fused_computation.26 | loop fusion | flops 2883584 | bytes 5455872 | tf_op jit(solution)/shard_map/div | solution.py:46
  27.1 0.4 fusion.24
  27.5 0.5 select_add_fusion.4
  28.0 0.4 fusion.23
  28.5 0.1 select_add_fusion.7
  28.8 0.1 multiply_add_fusion.4
  29.3 3.2 %add_multiply_fusion.2 = (f32[64,4,1024]{2,0,1:T(8,128)S(1)}, f32[64,4,1024]{2,0,1:T(8,128)}) fusion(f32[4,1024]{1,0:T(4,128)S(1)} %multiply_add_fusion.9, f32[64,1024]{1,0:T(8,128)S(1)} %multiply_add_fusion.4, f32[64,4,992]{2,0,1:T(8,128)S(1)} %get-tuple-element.38, f32[64,4,1024]{2,0,1:T(8,128)S(1)} %select_add_fusion.4, ...), kind=kLoop, calls=%fused_computation.21 | loop fusion | flops 2883584 | bytes 5455872 | tf_op jit(solution)/shard_map/div | solution.py:46
  32.5 0.4 fusion.22
  32.9 0.4 select_add_fusion.3
  33.3 0.4 fusion.21
  33.9 0.1 select_add_fusion.6
  34.1 0.1 multiply_add_fusion.3
  34.6 2.7 %multiply_reduce_fusion.6 = (f32[64,4]{0,1:T(4,128)S(1)}, f32[64,4,1024]{2,0,1:T(8,128)S(1)}) fusion(f32[4,1024]{1,0:T(4,128)S(1)} %multiply_add_fusion.8, f32[64,1024]{1,0:T(8,128)S(1)} %multiply_add_fusion.3, f32[64,4,992]{2,0,1:T(8,128)S(1)} %get-tuple-element.34, f32[64,4,1024]{2,0,1:T(8,128)S(1)} %select_add_fusion.3, ...), kind=kLoop, calls=%fused_computation.16 | loop fusion | flops 3145472 | bytes 4408320 | tf_op jit(solution)/shard_map/reduce_sum | solution.py:63
  37.3 0.9 fusion.6
  38.2 74.4 %all-gather = f32[2048,100]{1,0:T(8,128)S(1)} all-gather(f32[64,100]{1,0:T(8,128)S(1)} %fusion.6), channel_id=2, replica_groups=mesh['tgt'=8,'sup'=4] {'tgt','sup'}, dimensions={0}, use_global_device_ids=true | all-gather | bytes 844800 | tf_op jit(solution)/shard_map/all_gather | solution.py:103
  112.7 0.6 copy-done.8
  113.3 14.1 %all_gather.15 = f32[64,100]{1,0:T(8,128)S(1)} all-gather(f32[8,100]{1,0:T(8,128)S(1)} %fusion.5), channel_id=1, replica_groups=mesh['tgt'=8,'sup'=4] {'tgt'}, dimensions={0}, use_global_device_ids=true | all-gather | bytes 28800 | tf_op jit(solution)/shard_map/all_gather | solution.py:91
  127.4 0.8 fusion.8
  128.2 3.1 %multiply_reduce_fusion.2 = (f32[4,1024]{1,0:T(4,128)S(1)}, f32[64,4,1024]{2,0,1:T(8,128)S(1)}) fusion(f32[64,4,1024]{2,0,1:T(8,128)S(1)} %get-tuple-element.8, f32[64,4]{0,1:T(4,128)S(1)} %fusion.8, f32[4,1024]{1,0:T(4,128)S(1)} %multiply_add_fusion.8, f32[64,1024]{1,0:T(8,128)} %copy-done.3), kind=kLoop, calls=%fused_computation.3 | loop fusion | flops 2093056 | bytes 2393088 | tf_op jit(solution)/shard_map/reduce_sum | solution.py:71
  131.6 0.4 fusion.20
  132.0 0.4 select_add_fusion.2
  132.4 0.4 fusion.19
  132.8 0.8 copy-done.2
  133.6 2.3 %multiply_reduce_fusion.3 = (f32[4,1024]{1,0:T(4,128)S(1)}, f32[64,4,1024]{2,0,1:T(8,128)S(1)}) fusion(f32[64,4,1024]{2,0,1:T(8,128)S(1)} %copy-done.2, f32[4,1024]{1,0:T(4,128)S(1)} %multiply_add_fusion.9, f32[64,1024]{1,0:T(8,128)S(1)} %multiply_add_fusion.4, f32[64,4,992]{2,0,1:T(8,128)S(1)} %get-tuple-element.30, f32[64,4,1024]{2,0,1:T(8,128)S(1)} %select_add_fusion.2, ...), kind=kLoop, calls=%fused_computation.4 | loop fusion | flops 2879488 | bytes 5472256 | tf_op jit(solution)/shard_map/reduce_sum | solution.py:71
  136.2 0.4 fusion.18
  136.7 0.4 select_add_fusion.1
  137.1 0.4 fusion.17
  137.5 0.8 copy-done.1
  138.3 2.3 %multiply_reduce_fusion.4 = (f32[4,1024]{1,0:T(4,128)S(1)}, f32[64,4,1024]{2,0,1:T(8,128)S(1)}) fusion(f32[64,4,1024]{2,0,1:T(8,128)S(1)} %copy-done.1, f32[4,1024]{1,0:T(4,128)S(1)} %multiply_add_fusion.10, f32[64,1024]{1,0:T(8,128)S(1)} %multiply_add_fusion.5, f32[64,4,992]{2,0,1:T(8,128)S(1)} %get-tuple-element.26, ...), kind=kLoop, calls=%fused_computation.5 | loop fusion | flops 2879488 | bytes 5472256 | tf_op jit(solution)/shard_map/reduce_sum | solution.py:71
  141.0 0.4 fusion.16
  141.4 0.4 select_add_fusion
  141.8 0.4 fusion.15
  142.2 0.5 copy-done.4
  142.9 0.5 multiply_reduce_fusion.5
  143.6 0.6 pad_maximum_fusion
  144.2 0.6 constant_dynamic-slice_fusion
  (55 shorter events, 3.2 us)
Async XLA Ops:
  0.6 1.2 copy-start
  0.7 0.7 copy-start.9
  21.3 0.8 copy-start.7
  34.3 3.0 %copy-start.3 = (f32[64,1024]{1,0:T(8,128)}, f32[64,1024]{1,0:T(8,128)S(1)}, u32[]{:S(2)}) copy-start(f32[64,1024]{1,0:T(8,128)S(1)} %multiply_add_fusion.3) | copy-start | bytes 786436
  112.6 0.7 copy-start.8
  132.4 1.2 copy-start.2
  137.1 1.2 copy-start.1
  141.8 1.0 copy-start.4
  141.8 1.0 copy-start.5
  141.8 1.1 copy-start.6
